TPU v7x, 256 devices: a whole 4x4x8 slice. The times are simulated.
256 devices in a mesh: req: 32 (over x, z), head: 8 (over y, core).
Axes of the slice: x: 4, y: 4, z: 8, core: 2. Of those that a mesh axis runs over, the one named last changes fastest.
Arguments:
- tokens: bfloat16 [1024, 1280], P(('req', 'head')), may hold values from -6 to 6
- norm_attn: float32 [1280], replicated, may hold values from 0.1 to 1.9
- query_scale: float32 [80], replicated, may hold values from 0.05 to 0.2
- w_query: bfloat16 [1280, 1280], P('head'), may hold values from -0.15625 to 0.15625
- w_key: bfloat16 [1280, 1280], P('head'), may hold values from -0.15625 to 0.15625
- w_value: bfloat16 [1280, 1280], P('head'), may hold values from -0.15625 to 0.15625
- w_out: bfloat16 [1280, 1280], P('head'), may hold values from -0.15625 to 0.15625
- norm_mlp: float32 [1280], replicated, may hold values from 0.1 to 1.9
- w_up: bfloat16 [1280, 1280], P('req'), may hold values from -0.15625 to 0.15625
- w_down: bfloat16 [1280, 1280], P('req'), may hold values from -0.15625 to 0.15625
- cache_k: bfloat16 [1024, 1280, 512], P('req', 'head'), may hold values from -2000 to 2000
- cache_v: bfloat16 [1024, 1280, 512], P('req', 'head'), may hold values from -6 to 6
- lengths: int32 [1024], P('req'), may hold values from 1 to 512, as said below
Outputs:
- layer_out: bfloat16 [1024, 1280], P(('req', 'head'))
Inputs may be any that keep to these rules, and one draw needn't show every extreme that they name: `lengths`: each request has this many valid cache slots at the front of its 512; in every draw some request has all 512.
All inputs are finite; a program needn't handle non-finite values.
Results may differ from a plain program's by a relative error of at most 0.012.
The roundings to bfloat16 on the way count: a program that leaves them out, or rounds other values in their place, can miss the bound.
Values may be sent and summed in bfloat16 or wider, within the bound.
A program may use at most 128 MiB of HBM per device.

v0:
```python
import jax
import jax.numpy as jnp
from jax import lax
from jax.sharding import PartitionSpec as P


def rms_scale(values, gain):
    mean_sq = jnp.mean(values * values, axis=-1, keepdims=True)
    return values * lax.rsqrt(mean_sq + 1e-06) * gain


def times_rows(left, right):
    return lax.dot_general(
        left, right, (((1,), (1,)), ((), ())), preferred_element_type=jnp.float32
    )


def attend_whole(query, new_key, new_value, keys, values, lens):
    rows = query.shape[0]
    heads = query.shape[1]
    head_size = query.shape[2]
    slot_count = keys.shape[2]
    keys = keys.reshape(rows, heads, head_size, slot_count)
    values = values.reshape(rows, heads, head_size, slot_count)
    scores = jnp.einsum("rhd,rhdp->rhp", query, keys, preferred_element_type=jnp.float32)
    score_new = jnp.sum(query.astype(jnp.float32) * new_key.astype(jnp.float32), axis=-1)
    slots = jnp.arange(slot_count, dtype=jnp.int32)
    valid = slots[None, None, :] < lens[:, None, None]
    top = jnp.maximum(jnp.max(jnp.where(valid, scores, -jnp.inf), axis=-1), score_new)
    weights = jnp.where(valid, jnp.exp(scores - top[..., None]), 0.0)
    weight_new = jnp.exp(score_new - top)
    total = jnp.sum(weights, axis=-1) + weight_new
    probs = weights.astype(jnp.bfloat16)
    prob_new = weight_new.astype(jnp.bfloat16).astype(jnp.float32)
    summed = jnp.einsum("rhp,rhdp->rhd", probs, values, preferred_element_type=jnp.float32)
    summed = summed + prob_new[..., None] * new_value.astype(jnp.float32)
    result = (summed / total[..., None]).astype(jnp.bfloat16)
    return result.reshape(rows, heads * head_size)


def shards(
    tokens,
    norm_attn,
    query_scale,
    w_query,
    w_key,
    w_value,
    w_out,
    norm_mlp,
    w_up,
    w_down,
    cache_k,
    cache_v,
    lengths,
):
    head_size = query_scale.shape[0]
    local_feats = w_query.shape[0]
    heads_here = local_feats // head_size
    inputs = tokens.astype(jnp.float32)
    normed = rms_scale(inputs, norm_attn).astype(jnp.bfloat16)
    piece = lax.all_gather(normed, "head", axis=0, tiled=True)
    projected = jnp.concatenate(
        [times_rows(piece, w_query), times_rows(piece, w_key), times_rows(piece, w_value)], axis=1
    )
    group_rows = projected.shape[0]
    query = projected[:, :local_feats].reshape(group_rows, heads_here, head_size)
    query = (query * query_scale).astype(jnp.bfloat16)
    new_key = (
        projected[:, local_feats : 2 * local_feats]
        .astype(jnp.bfloat16)
        .reshape(group_rows, heads_here, head_size)
    )
    new_value = (
        projected[:, 2 * local_feats :]
        .astype(jnp.bfloat16)
        .reshape(group_rows, heads_here, head_size)
    )
    attended = attend_whole(query, new_key, new_value, cache_k, cache_v, lengths)
    part_rows = attended
    mid = inputs + lax.psum_scatter(
        jnp.dot(part_rows, w_out, preferred_element_type=jnp.float32),
        "head",
        scatter_dimension=0,
        tiled=True,
    )
    normed_mid = rms_scale(mid, norm_mlp).astype(jnp.bfloat16)
    all_rows = lax.all_gather(normed_mid, "req", axis=0, tiled=True)
    part_rows = all_rows
    hidden = jax.nn.silu(times_rows(part_rows, w_up)).astype(jnp.bfloat16)
    mixed = lax.psum_scatter(
        jnp.dot(hidden, w_down, preferred_element_type=jnp.float32),
        "req",
        scatter_dimension=0,
        tiled=True,
    )
    return (mid + mixed).astype(jnp.bfloat16)


def solution(mesh):
    in_specs = (
        P(("req", "head"), None),
        P(),
        P(),
        P("head", None),
        P("head", None),
        P("head", None),
        P("head", None),
        P(),
        P("req", None),
        P("req", None),
        P("req", "head", None),
        P("req", "head", None),
        P("req"),
    )
    out_specs = P(("req", "head"), None)
    return jax.shard_map(shards, mesh=mesh, in_specs=in_specs, out_specs=out_specs, check_vma=False)
```

profile of v0, /device:TPU:1, one launch (start us, length us, event | category | flops | bytes accessed | tf_op | source)
XLA Modules:
  0.0 305.9 jit_solution(17118482060196402668)
XLA Ops:
  6.5 0.9 fusion.13
  7.4 0.7 iota_compare_fusion
  8.2 0.8 fusion.19
  9.0 15.8 %all-gather = bf16[8,4,1280]{2,1,0:T(4,128)(2,1)S(1)} all-gather(bf16[1,4,1280]{2,1,0:T(4,128)(2,1)S(1)} %fusion.19), channel_id=1, replica_groups=mesh['req'=32,'head'=8] {'head'}, dimensions={0}, use_global_device_ids=true | all-gather | bytes 92160 | tf_op jit(solution)/shard_map/all_gather | solution.py:61
  24.8 1.2 fusion
  26.0 0.2 reshape.83
  26.1 1.2 fusion.1
  27.3 1.3 fusion.26
  28.6 0.2 reshape.78
  28.8 0.8 multiply_reduce_fusion
  29.7 3.3 %fusion.10 = f32[32,2,1,512]{3,2,1,0:T(1,128)S(1)} fusion(bf16[32,2,80,512]{3,2,1,0:T(8,128)(2,1)} %bitcast.42, bf16[32,2,80,1]{2,1,0,3:T(2,128)(2,1)S(1)} %get-tuple-element.10), kind=kOutput, calls=%fused_computation.15 | convolution fusion | flops 5242880 | bytes 5384192 | tf_op jit(solution)/shard_map/rhd,rhdp->rhp/dot_general | solution.py:25
  33.1 0.2 fusion.7
  33.5 3.9 %fusion.5 = f32[32,2,1,80]{3,2,1,0:T(1,128)S(1)} fusion(bf16[32,2,80,512]{3,2,1,0:T(8,128)(2,1)} %bitcast.44, bf16[32,2,512,1]{2,0,1,3:T(8,128)(2,1)S(1)} %get-tuple-element.8), kind=kOutput, calls=%fused_computation.9 | convolution fusion | flops 5242880 | bytes 5328896 | tf_op jit(solution)/shard_map/rhp,rhdp->rhd/dot_general | solution.py:35
  37.5 0.2 fusion.12
  37.7 0.9 fusion.27
  38.7 0.6 dynamic-slice
  39.9 62.6 %all-reduce.5.cloned.1.call-done = f32[32,1280]{1,0:T(8,128)} async-done(((f32[32,1280]{1,0:T(8,128)}), f32[32,1280]{1,0:T(8,128)}) %all-reduce.5.cloned.1.call-update) | async-done | bytes 163856
  102.5 0.9 multiply_reduce_fusion.1
  103.4 0.9 fusion.18
  104.3 38.4 %all-gather.1 = bf16[32,4,1280]{2,1,0:T(4,128)(2,1)S(1)} all-gather(bf16[1,4,1280]{2,1,0:T(4,128)(2,1)S(1)} %fusion.18), channel_id=1, replica_groups=mesh['req'=32,'head'=8] {'req'}, dimensions={0}, use_global_device_ids=true | all-gather | bytes 337920 | tf_op jit(solution)/shard_map/all_gather | solution.py:87
  142.8 1.5 fusion.17
  144.3 0.6 dynamic-slice.2
  145.5 152.1 %all-reduce.7.cloned.1.call-done = f32[128,1280]{1,0:T(8,128)} async-done(((f32[128,1280]{1,0:T(8,128)}), f32[128,1280]{1,0:T(8,128)}) %all-reduce.7.cloned.1.call-update) | async-done | bytes 655376
  297.6 1.4 fusion.16
  (30 shorter events, 0.8 us)
Async XLA Ops:
  6.5 31.2 %copy-start = (bf16[160,1280]{1,0:T(8,128)(2,1)S(1)}, bf16[160,1280]{1,0:T(8,128)(2,1)}, u32[]{:S(2)}) copy-start(bf16[160,1280]{1,0:T(8,128)(2,1)} %param.19) | copy-start | bytes 1228804
  6.5 95.9 %all-reduce.5.cloned.1.call-start = ((), (), s32[]{:S(2)}) async-start(), calls=%async_computation | async-start | bytes 327680
  29.7 9.0 %copy-start.6 = (u32[256]{0:T(256)S(1)}, u32[256]{0:T(256)}, u32[]{:S(2)}) copy-start(u32[256]{0:T(256)} %constant.18) | copy-start | bytes 3076
  29.7 72.8 %copy-start.1 = (bf16[4,1280]{1,0:T(4,128)(2,1)S(1)}, bf16[4,1280]{1,0:T(4,128)(2,1)}, u32[]{:S(2)}) copy-start(bf16[4,1280]{1,0:T(4,128)(2,1)} %param.13) | copy-start | bytes 30724
  29.7 73.7 %copy-start.4 = (f32[1280]{0:T(1024)S(1)}, f32[1280]{0:T(1024)}, u32[]{:S(2)}) copy-start(f32[1280]{0:T(1024)} %param.20) | copy-start | bytes 15364
  33.0 109.7 %copy-start.2 = (bf16[40,1280]{1,0:T(8,128)(2,1)S(1)}, bf16[40,1280]{1,0:T(8,128)(2,1)}, u32[]{:S(2)}) copy-start(bf16[40,1280]{1,0:T(8,128)(2,1)} %param.22) | copy-start | bytes 307204
  33.0 109.7 %copy-start.3 = (bf16[40,1280]{1,0:T(8,128)(2,1)S(1)}, bf16[40,1280]{1,0:T(8,128)(2,1)}, u32[]{:S(2)}) copy-start(bf16[40,1280]{1,0:T(8,128)(2,1)} %param.21) | copy-start | bytes 307204
  33.0 111.3 %copy-start.5 = (u32[256]{0:T(256)S(1)}, u32[256]{0:T(256)}, u32[]{:S(2)}) copy-start(u32[256]{0:T(256)} %constant.22) | copy-start | bytes 3076
  38.6 259.1 %all-reduce.7.cloned.1.call-start = ((), (), s32[]{:S(2)}) async-start(), calls=%async_computation.1 | async-start | bytes 1310720
Sparse Core Ops, SparseCore 0:
  38.7 63.7 all-reduce.4
  144.4 153.1 all-reduce.6
where the time goes:
time: 310 us; the launch traced here: 306 us
  waiting for transfers between devices  215 us (69%)
  blocking collectives  54.2 us (17%)
  between operations  14.8 us (5%)
  matrix products  13.2 us (4%)
  other arithmetic  6.84 us (2%)
    unnamed x4, waiting for transfers between devices  215 us
    all_gather x1, blocking collectives, shards(): all_rows = lax.all_gather(normed_mid, 'req', axis=0, tiled=True)  38.4 us
    all_gather x1, blocking collectives, shards(): piece = lax.all_gather(normed, 'head', axis=0, tiled=True)  15.8 us
  transfers between devices with their start and end apart: 2, of which 2 were waited for; matrix products, arithmetic and copies ran while one was open for 0% of the time, Pallas kernels for 0%

commit v1 on v0

v1 whole, which is shorter than its diff:
```python
import jax
import jax.numpy as jnp
from jax import lax
from jax.experimental import pallas as pl
from jax.experimental.pallas import tpu as pltpu
from jax.sharding import PartitionSpec as P

MESH = pl.DeviceIdType.MESH
D = 1280
HD = 80
FEATS = 160
ROWS = 32
CACHE = 512
OWN = 4
HEADS = 8
PEERS = 16
UNITS = 40
F32 = jnp.float32
BF16 = jnp.bfloat16


def rms_scale(values, gain):
    mean_sq = jnp.mean(values * values, axis=-1, keepdims=True)
    return values * lax.rsqrt(mean_sq + 1e-06) * gain


def times_rows(left, right):
    return lax.dot_general(left, right, (((1,), (1,)), ((), ())), preferred_element_type=F32)


def times(left, right):
    return lax.dot_general(left, right, (((1,), (0,)), ((), ())), preferred_element_type=F32)


def layer(
    tok_hbm, gain_attn_ref, scale_ref, wq_hbm, wk_hbm, wv_hbm, wo_hbm, gain_mlp_ref, wu_hbm, wd_hbm,
    ck_hbm, cv_hbm, lens_ref, out_ref,
    tok_buf, rows_buf, wq_buf, wk_buf, wv_buf, wo_buf, k_buf, v_buf, wu_buf, wd_buf, spread_buf, att_buf,
    part_send, part_recv, nm_buf, nm_rows, ff_send, ff_recv,
    load_sem, k_sem, v_sem,
    tok_ssem, tok_rsem, part_ssem, part_rsem, nm_ssem, nm_rsem, ff_ssem, ff_rsem, w_ssem, w_rsem,
):
    me_req = lax.axis_index("req")
    me_head = lax.axis_index("head")
    x = me_req // 8
    z = me_req % 8
    y = me_head // 2
    core = me_head % 2
    place = x * 4 + (z % 2) * 2 + core

    def head_peer(k):
        return (me_req, (me_head + k) % HEADS)

    def near_peer(k):
        at = (place + k) % PEERS
        return ((at // 4) * 8 + (z // 2) * 2 + (at // 2) % 2, y * 2 + at % 2)

    def z_peer(k, at_core):
        return (x * 8 + (z + k) % 8, y * 2 + at_core)

    load_tok = pltpu.make_async_copy(tok_hbm, tok_buf.at[me_head], load_sem.at[0])
    load_tok.start()
    loads = []
    for n, (src, dst) in enumerate(((wq_hbm, wq_buf), (wk_hbm, wk_buf), (wv_hbm, wv_buf))):
        loads.append(pltpu.make_async_copy(src, dst, load_sem.at[1 + n]))
        loads[-1].start()
    load_k, load_v = [], []
    for g in range(4):
        rows = pl.ds(g * D, D)
        load_k.append(pltpu.make_async_copy(ck_hbm.at[rows], k_buf.at[rows], k_sem.at[g]))
        load_k[-1].start()
    for g in range(4):
        rows = pl.ds(g * D, D)
        load_v.append(pltpu.make_async_copy(cv_hbm.at[rows], v_buf.at[rows], v_sem.at[g]))
        load_v[-1].start()
    load_wo = pltpu.make_async_copy(wo_hbm, wo_buf, load_sem.at[4])
    load_wo.start()
    load_wu = pltpu.make_async_copy(wu_hbm, wu_buf.at[0], load_sem.at[5])
    load_wd = pltpu.make_async_copy(wd_hbm, wd_buf.at[0], load_sem.at[6])

    barrier = pltpu.get_barrier_semaphore()
    for k in range(1, HEADS):
        pl.semaphore_signal(barrier, inc=1, device_id=head_peer(k), device_id_type=MESH)
    for k in range(1, PEERS):
        pl.semaphore_signal(barrier, inc=1, device_id=near_peer(k), device_id_type=MESH)
    for k in (2, 6):
        pl.semaphore_signal(barrier, inc=1, device_id=z_peer(k, 1 - core), device_id_type=MESH)

    column = lax.broadcasted_iota(jnp.int32, (1, D), 1)
    block = jnp.zeros((1, D), jnp.int32)
    for n in range(1, 8):
        block = block + (column >= n * FEATS).astype(jnp.int32)
    feature = column - block * FEATS
    feature_rows = lax.broadcasted_iota(jnp.int32, (FEATS, D), 0)
    spread_buf[...] = jnp.where(feature_rows == feature, 1.0, 0.0).astype(BF16)
    request = lax.broadcasted_iota(jnp.int32, (8, D), 0)
    masks = (
        (request == block) & (feature < HD),
        (request == block) & (feature >= HD),
    )

    load_tok.wait()
    pl.semaphore_wait(barrier, HEADS - 1 + PEERS - 1 + 2)

    def remote(src, dst, ssem, rsem, device):
        return pltpu.make_async_remote_copy(
            src_ref=src, dst_ref=dst, send_sem=ssem, recv_sem=rsem, device_id=device, device_id_type=MESH
        )

    tok_out = []
    for k in range(1, HEADS):
        copy = remote(
            tok_buf.at[me_head], tok_buf.at[me_head], tok_ssem.at[k], tok_rsem.at[k], head_peer(k)
        )
        copy.start()
        tok_out.append(copy)

    def shard_copies(n, k):
        return (
            remote(wu_hbm, wu_buf.at[n], w_ssem.at[2 * n], w_rsem.at[2 * n], z_peer(k, 1)),
            remote(wd_hbm, wd_buf.at[n], w_ssem.at[2 * n + 1], w_rsem.at[2 * n + 1], z_peer(k, 1)),
        )

    def passed_on():
        return (
            remote(wu_buf.at[0], wu_buf.at[1], w_ssem.at[0], w_rsem.at[2], z_peer(6, 0)),
            remote(wd_buf.at[1], wd_buf.at[1], w_ssem.at[1], w_rsem.at[3], z_peer(2, 0)),
        )

    @pl.when(core == 0)
    def _():
        for n, k in ((0, 6), (1, 2)):
            for copy in shard_copies(n, k):
                copy.start()
        load_wu.start()
        load_wd.start()

    for copy in tok_out:
        copy.wait_recv()
    for n in range(HEADS):
        rows_buf[pl.ds(OWN * n, OWN), :] = tok_buf[n].astype(F32)
    normed = rms_scale(rows_buf[...], gain_attn_ref[...]).astype(BF16)

    for copy in loads:
        copy.wait()
    scale = scale_ref[...]
    scale = jnp.concatenate([scale, scale], axis=1)
    query = (times_rows(normed, wq_buf[...]) * scale).astype(BF16)
    new_key = times_rows(normed, wk_buf[...]).astype(BF16)
    new_value = times_rows(normed, wv_buf[...]).astype(BF16)
    spread_query = times(query, spread_buf[...])
    spread_value = times(new_value, spread_buf[...])
    product = query.astype(F32) * new_key.astype(F32)
    lane = lax.broadcasted_iota(jnp.int32, (ROWS, FEATS), 1)
    score_new = (
        jnp.sum(jnp.where(lane < HD, product, 0.0), axis=-1, keepdims=True),
        jnp.sum(jnp.where(lane >= HD, product, 0.0), axis=-1, keepdims=True),
    )
    eye = lax.broadcasted_iota(jnp.int32, (ROWS, ROWS), 0) == lax.broadcasted_iota(jnp.int32, (ROWS, ROWS), 1)
    lens = jnp.sum(jnp.where(eye, jnp.broadcast_to(lens_ref[...], (ROWS, ROWS)), 0), axis=-1, keepdims=True)

    slot = lax.broadcasted_iota(jnp.int32, (16, CACHE), 1)
    scores = []
    for g in range(4):
        at = slice(8 * g, 8 * g + 8)
        load_k[g].wait()
        left = jnp.concatenate([jnp.where(mask, spread_query[at], 0.0) for mask in masks], axis=0)
        scores.append(times(left.astype(BF16), k_buf[pl.ds(g * D, D), :]))
    probs, prob_new, total = [], [], []
    for g in range(4):
        at = slice(8 * g, 8 * g + 8)
        fresh = jnp.concatenate([score_new[0][at], score_new[1][at]], axis=0)
        length = jnp.concatenate([lens[at], lens[at]], axis=0)
        valid = slot < length
        top = jnp.maximum(jnp.max(jnp.where(valid, scores[g], -jnp.inf), axis=-1, keepdims=True), fresh)
        weights = jnp.where(valid, jnp.exp(scores[g] - top), 0.0)
        weight_new = jnp.exp(fresh - top)
        total.append(jnp.sum(weights, axis=-1, keepdims=True) + weight_new)
        probs.append(weights.astype(BF16))
        prob_new.append(weight_new.astype(BF16).astype(F32))
    for g in range(4):
        at = slice(8 * g, 8 * g + 8)
        load_v[g].wait()
        summed = times_rows(probs[g], v_buf[pl.ds(g * D, D), :])
        picked = jnp.zeros((8, D), F32)
        for h in range(2):
            half = slice(8 * h, 8 * h + 8)
            result = (summed[half] + prob_new[g][half] * spread_value[at]) / total[g][half]
            picked = jnp.where(masks[h], result, picked)
        att_buf[pl.ds(8 * g, 8), :] = picked
    attended = times_rows(att_buf[...].astype(BF16), spread_buf[...]).astype(BF16)
    load_wo.wait()
    part = times(attended, wo_buf[...])
    for n in range(HEADS):
        part_send[n] = part[OWN * n : OWN * n + OWN].astype(BF16)
    part_out = []
    for k in range(1, HEADS):
        copy = remote(
            part_send.at[(me_head + k) % HEADS], part_recv.at[k], part_ssem.at[k], part_rsem.at[k], head_peer(k)
        )
        copy.start()
        part_out.append(copy)

    @pl.when(core == 1)
    def _():
        for n, k in ((0, 6), (1, 2)):
            for copy in shard_copies(n, k):
                copy.wait_recv()
        for copy in passed_on():
            copy.start()

    mid = tok_buf[me_head].astype(F32)
    mid = mid + part_send[me_head].astype(F32)
    for k, copy in enumerate(part_out, start=1):
        copy.wait_recv()
        mid = mid + part_recv[k].astype(F32)
    nm_buf[0] = rms_scale(mid, gain_mlp_ref[...]).astype(BF16)
    nm_out = []
    for k in range(1, PEERS):
        copy = remote(nm_buf.at[0], nm_buf.at[k], nm_ssem.at[k], nm_rsem.at[k], near_peer(k))
        copy.start()
        nm_out.append(copy)

    @pl.when(core == 0)
    def _():
        load_wu.wait()
        load_wd.wait()
        for copy in passed_on():
            copy.wait_recv()

    for copy in nm_out:
        copy.wait_recv()
    for n in range(PEERS):
        nm_rows[pl.ds(OWN * n, OWN), :] = nm_buf[n].astype(F32)
    normed_mid = nm_rows[...].astype(BF16)
    mixed = jnp.zeros((PEERS * OWN, D), F32)
    for n in range(2):
        hidden = times_rows(normed_mid, wu_buf[n])
        hidden = (hidden / (1.0 + jnp.exp(-hidden))).astype(BF16)
        mixed = mixed + times(hidden, wd_buf[n])
    for n in range(PEERS):
        ff_send[n] = mixed[OWN * n : OWN * n + OWN].astype(BF16)
    ff_out = []
    for k in range(1, PEERS):
        copy = remote(ff_send.at[PEERS - k], ff_recv.at[k], ff_ssem.at[k], ff_rsem.at[k], near_peer(k))
        copy.start()
        ff_out.append(copy)
    result = mid + ff_send[0].astype(F32)
    for k, copy in enumerate(ff_out, start=1):
        copy.wait_recv()
        result = result + ff_recv[k].astype(F32)
    out_ref[...] = result.astype(BF16)

    for copy in tok_out + part_out + nm_out + ff_out:
        copy.wait_send()

    @pl.when(core == 0)
    def _():
        for n, k in ((0, 6), (1, 2)):
            for copy in shard_copies(n, k):
                copy.wait_send()

    @pl.when(core == 1)
    def _():
        for copy in passed_on():
            copy.wait_send()


def shards(
    tokens, norm_attn, query_scale, w_query, w_key, w_value, w_out, norm_mlp, w_up, w_down, cache_k, cache_v, lengths
):
    anywhere = pl.BlockSpec(memory_space=pl.ANY)
    vmem = pl.BlockSpec(memory_space=pltpu.VMEM)
    dma = pltpu.SemaphoreType.DMA
    return pl.pallas_call(
        layer,
        out_shape=jax.ShapeDtypeStruct((OWN, D), BF16),
        in_specs=[anywhere, vmem, vmem, anywhere, anywhere, anywhere, anywhere, vmem]
        + [anywhere] * 4 + [vmem],
        out_specs=vmem,
        scratch_shapes=[
            pltpu.VMEM((HEADS, OWN, D), BF16),
            pltpu.VMEM((ROWS, D), F32),
            pltpu.VMEM((FEATS, D), BF16),
            pltpu.VMEM((FEATS, D), BF16),
            pltpu.VMEM((FEATS, D), BF16),
            pltpu.VMEM((FEATS, D), BF16),
            pltpu.VMEM((ROWS * FEATS, CACHE), BF16),
            pltpu.VMEM((ROWS * FEATS, CACHE), BF16),
            pltpu.VMEM((2, UNITS, D), BF16),
            pltpu.VMEM((2, UNITS, D), BF16),
            pltpu.VMEM((FEATS, D), BF16),
            pltpu.VMEM((ROWS, D), F32),
            pltpu.VMEM((HEADS, OWN, D), BF16),
            pltpu.VMEM((HEADS, OWN, D), BF16),
            pltpu.VMEM((PEERS, OWN, D), BF16),
            pltpu.VMEM((PEERS * OWN, D), F32),
            pltpu.VMEM((PEERS, OWN, D), BF16),
            pltpu.VMEM((PEERS, OWN, D), BF16),
            dma((7,)), dma((4,)), dma((4,)),
            dma((HEADS,)), dma((HEADS,)), dma((HEADS,)), dma((HEADS,)),
            dma((PEERS,)), dma((PEERS,)), dma((PEERS,)), dma((PEERS,)),
            dma((4,)), dma((4,)),
        ],
        compiler_params=pltpu.CompilerParams(
            collective_id=0, has_side_effects=True, vmem_limit_bytes=60 * 1024 * 1024
        ),
        name="decode_layer",
    )(
        tokens, norm_attn.reshape(1, D), query_scale.reshape(1, HD), w_query, w_key, w_value, w_out,
        norm_mlp.reshape(1, D), w_up, w_down, cache_k.reshape(ROWS * FEATS, CACHE),
        cache_v.reshape(ROWS * FEATS, CACHE), lengths.reshape(1, ROWS),
    )


def solution(mesh):
    in_specs = (
        P(("req", "head"), None),
        P(),
        P(),
        P("head", None),
        P("head", None),
        P("head", None),
        P("head", None),
        P(),
        P("req", None),
        P("req", None),
        P("req", "head", None),
        P("req", "head", None),
        P("req"),
    )
    out_specs = P(("req", "head"), None)
    return jax.shard_map(shards, mesh=mesh, in_specs=in_specs, out_specs=out_specs, check_vma=False)
```

time: 310 us -> 37.9 us (0.12); the launches traced: 306 us -> 37.7 us
  waiting for transfers between devices: 215 us -> 0 us
  blocking collectives: 54.2 us -> 0 us
  Pallas kernels: 0 us -> 33.8 us
  between operations: 14.8 us -> 0.01 us
  matrix products: 13.2 us -> 0 us
  other arithmetic: 6.84 us -> 0 us
    unnamed x4 -> x0, waiting for transfers between devices: 215 us -> none
    all_gather x2 -> x0, blocking collectives: 54.2 us -> none  [the longest x1 38.4 us: shards(): all_rows = lax.all_gather(normed_mid, 'req', axis=0, tiled=True)]
    pallas_call x0 -> x1, Pallas kernels: none -> 33.8 us  [shards(): pl.pallas_call(layer, out_shape=jax.ShapeDtypeStruct((OWN, D), BF16), in_...]
    dot_general x7 -> x0, matrix products: 13.2 us -> none  [the longest x1 3.94 us: attend_whole(): jnp.einsum('rhp,rhdp->rhd', probs, values, preferred_element_type=jnp.flo...]
  transfers between devices with their start and end apart: 2 -> 0, of which waited for: 2 -> 0; matrix products, arithmetic and copies ran while one was open for 0% -> 0% of each run, Pallas kernels for 0% -> 0%
where the time goes in v1:
time: 37.9 us; the launch traced here: 37.7 us
  Pallas kernels  33.8 us (89%)
  local copies, waits for them, and re-layouts  3.89 us (10%)
    pallas_call x1, Pallas kernels, shards(): pl.pallas_call(layer, out_shape=jax.ShapeDtypeStruct((OWN, D), BF16), in_...  33.8 us
    unnamed x1, local copies, waits for them, and re-layouts  1.31 us
    reshape x1, local copies, waits for them, and re-layouts, shards(): norm_attn.reshape(1, D)  1.29 us
    reshape x1, local copies, waits for them, and re-layouts, shards(): norm_mlp.reshape(1, D)  1.29 us

profile of v1, /device:TPU:1, one launch (start us, length us, event | category | flops | bytes accessed | tf_op | source)
XLA Modules:
  0.0 37.7 jit_solution(6089841693362997021)
XLA Ops:
  0.0 1.3 %reshape.18.gain_attn_ref = f32[1,1280]{1,0:T(1,128)} reshape(f32[1280]{0:T(1024)} %param.14) | data formatting | bytes 10240 | tf_op jit(solution)/shard_map/reshape | solution.py:310
  1.3 1.3 %reshape.20.gain_mlp_ref = f32[1,1280]{1,0:T(1,128)} reshape(f32[1280]{0:T(1024)} %param.20) | data formatting | bytes 10240 | tf_op jit(solution)/shard_map/reshape | solution.py:311
  2.6 33.8 %decode_layer.1 = bf16[4,1280]{1,0:T(4,128)(2,1)} custom-call(bf16[4,1280]{1,0:T(4,128)(2,1)} %tok_hbm.1, f32[1,1280]{1,0:T(1,128)} %reshape.18.gain_attn_ref, f32[1,80]{1,0:T(1,128)} %bitcast.6, bf16[160,1280]{1,0:T(8,128)(2,1)} %wq_hbm.1, bf16[160,1280]{1,0:T(8,128)(2,1)} %wk_hbm.1, bf16[160,1280]{1,0:T(8,128)(2,1)} %wv_hbm.1, bf16[160,1280]{1,0:T(8,128)(2,1)} %wo_hbm.1, ...), custom_call_target="tpu_custom_call" | custom-call | tf_op jit(solution)/shard_map/decode_layer/pallas_call | solution.py:275
  36.4 1.3 %copy.15 = bf16[4,1280]{1,0:T(4,128)(2,1)} copy(bf16[4,1280]{1,0:T(4,128)(2,1)} %decode_layer.1) | data formatting | bytes 20480

commit v2 on v1

--- a/solution.py
+++ b/solution.py
@@ -33,11 +33,12 @@
 
 
 def layer(
-    tok_hbm, gain_attn_ref, scale_ref, wq_hbm, wk_hbm, wv_hbm, wo_hbm, gain_mlp_ref, wu_hbm, wd_hbm,
-    ck_hbm, cv_hbm, lens_ref, out_ref,
+    tok_hbm, gain_attn_hbm, scale_hbm, wq_hbm, wk_hbm, wv_hbm, wo_hbm, gain_mlp_hbm, wu_hbm, wd_hbm,
+    ck_hbm, cv_hbm, lens_hbm, out_hbm,
+    gain_attn_ref, scale_ref, gain_mlp_ref, lens_ref, out_ref,
     tok_buf, rows_buf, wq_buf, wk_buf, wv_buf, wo_buf, k_buf, v_buf, wu_buf, wd_buf, spread_buf, att_buf,
     part_send, part_recv, nm_buf, nm_rows, ff_send, ff_recv,
-    load_sem, k_sem, v_sem,
+    load_sem, small_sem, k_sem, v_sem, ready_sem,
     tok_ssem, tok_rsem, part_ssem, part_rsem, nm_ssem, nm_rsem, ff_ssem, ff_rsem, w_ssem, w_rsem,
 ):
     me_req = lax.axis_index("req")
@@ -58,8 +59,25 @@
     def z_peer(k, at_core):
         return (x * 8 + (z + k) % 8, y * 2 + at_core)
 
+    later = (z < 6, z < 2)
+    barrier = pltpu.get_barrier_semaphore()
+    for k in range(1, HEADS):
+        pl.semaphore_signal(barrier, inc=1, device_id=head_peer(k), device_id_type=MESH)
+    for k in range(1, PEERS):
+        pl.semaphore_signal(barrier, inc=1, device_id=near_peer(k), device_id_type=MESH)
+    for n, k in enumerate((2, 6)):
+        @pl.when(later[n])
+        def _():
+            pl.semaphore_signal(barrier, inc=1, device_id=z_peer(k, 1 - core), device_id_type=MESH)
+
     load_tok = pltpu.make_async_copy(tok_hbm, tok_buf.at[me_head], load_sem.at[0])
     load_tok.start()
+    smalls = []
+    for n, (src, dst) in enumerate((
+        (gain_attn_hbm, gain_attn_ref), (scale_hbm, scale_ref), (lens_hbm, lens_ref), (gain_mlp_hbm, gain_mlp_ref)
+    )):
+        smalls.append(pltpu.make_async_copy(src, dst, small_sem.at[n]))
+        smalls[-1].start()
     loads = []
     for n, (src, dst) in enumerate(((wq_hbm, wq_buf), (wk_hbm, wk_buf), (wv_hbm, wv_buf))):
         loads.append(pltpu.make_async_copy(src, dst, load_sem.at[1 + n]))
@@ -77,14 +95,6 @@
     load_wo.start()
     load_wu = pltpu.make_async_copy(wu_hbm, wu_buf.at[0], load_sem.at[5])
     load_wd = pltpu.make_async_copy(wd_hbm, wd_buf.at[0], load_sem.at[6])
-
-    barrier = pltpu.get_barrier_semaphore()
-    for k in range(1, HEADS):
-        pl.semaphore_signal(barrier, inc=1, device_id=head_peer(k), device_id_type=MESH)
-    for k in range(1, PEERS):
-        pl.semaphore_signal(barrier, inc=1, device_id=near_peer(k), device_id_type=MESH)
-    for k in (2, 6):
-        pl.semaphore_signal(barrier, inc=1, device_id=z_peer(k, 1 - core), device_id_type=MESH)
 
     column = lax.broadcasted_iota(jnp.int32, (1, D), 1)
     block = jnp.zeros((1, D), jnp.int32)
@@ -100,7 +110,7 @@
     )
 
     load_tok.wait()
-    pl.semaphore_wait(barrier, HEADS - 1 + PEERS - 1 + 2)
+    pl.semaphore_wait(barrier, HEADS - 1 + PEERS - 1 + (z >= 2).astype(jnp.int32) + (z >= 6).astype(jnp.int32))
 
     def remote(src, dst, ssem, rsem, device):
         return pltpu.make_async_remote_copy(
@@ -127,11 +137,28 @@
             remote(wd_buf.at[1], wd_buf.at[1], w_ssem.at[1], w_rsem.at[3], z_peer(2, 0)),
         )
 
+    for n, k in enumerate((2, 6)):
+        @pl.when(jnp.logical_not(later[n]))
+        def _():
+            pl.semaphore_signal(ready_sem.at[1 - n], inc=1, device_id=z_peer(k, 1 - core), device_id_type=MESH)
+
+            @pl.when(core == 0)
+            def _():
+                for copy in shard_copies(1 - n, k):
+                    copy.start()
+
+    def send_later(n, k):
+        @pl.when(later[n])
+        def _():
+            pl.semaphore_wait(ready_sem.at[n], 1)
+
+            @pl.when(core == 0)
+            def _():
+                for copy in shard_copies(1 - n, k):
+                    copy.start()
+
     @pl.when(core == 0)
     def _():
-        for n, k in ((0, 6), (1, 2)):
-            for copy in shard_copies(n, k):
-                copy.start()
         load_wu.start()
         load_wd.start()
 
@@ -139,7 +166,9 @@
         copy.wait_recv()
     for n in range(HEADS):
         rows_buf[pl.ds(OWN * n, OWN), :] = tok_buf[n].astype(F32)
-    normed = rms_scale(rows_buf[...], gain_attn_ref[...]).astype(BF16)
+    for copy in smalls:
+        copy.wait()
+    normed = rms_scale(rows_buf[...], gain_attn_ref[...].reshape(1, D)).astype(BF16)
 
     for copy in loads:
         copy.wait()
@@ -159,6 +188,7 @@
     eye = lax.broadcasted_iota(jnp.int32, (ROWS, ROWS), 0) == lax.broadcasted_iota(jnp.int32, (ROWS, ROWS), 1)
     lens = jnp.sum(jnp.where(eye, jnp.broadcast_to(lens_ref[...], (ROWS, ROWS)), 0), axis=-1, keepdims=True)
 
+    send_later(0, 2)
     slot = lax.broadcasted_iota(jnp.int32, (16, CACHE), 1)
     scores = []
     for g in range(4):
@@ -201,6 +231,8 @@
         copy.start()
         part_out.append(copy)
 
+    send_later(1, 6)
+
     @pl.when(core == 1)
     def _():
         for n, k in ((0, 6), (1, 2)):
@@ -214,7 +246,7 @@
     for k, copy in enumerate(part_out, start=1):
         copy.wait_recv()
         mid = mid + part_recv[k].astype(F32)
-    nm_buf[0] = rms_scale(mid, gain_mlp_ref[...]).astype(BF16)
+    nm_buf[0] = rms_scale(mid, gain_mlp_ref[...].reshape(1, D)).astype(BF16)
     nm_out = []
     for k in range(1, PEERS):
         copy = remote(nm_buf.at[0], nm_buf.at[k], nm_ssem.at[k], nm_rsem.at[k], near_peer(k))
@@ -250,6 +282,8 @@
         copy.wait_recv()
         result = result + ff_recv[k].astype(F32)
     out_ref[...] = result.astype(BF16)
+    store_out = pltpu.make_async_copy(out_ref, out_hbm, load_sem.at[7])
+    store_out.start()
 
     for copy in tok_out + part_out + nm_out + ff_out:
         copy.wait_send()
@@ -264,21 +298,26 @@
     def _():
         for copy in passed_on():
             copy.wait_send()
+
+    store_out.wait()
 
 
 def shards(
     tokens, norm_attn, query_scale, w_query, w_key, w_value, w_out, norm_mlp, w_up, w_down, cache_k, cache_v, lengths
 ):
     anywhere = pl.BlockSpec(memory_space=pl.ANY)
-    vmem = pl.BlockSpec(memory_space=pltpu.VMEM)
     dma = pltpu.SemaphoreType.DMA
     return pl.pallas_call(
         layer,
         out_shape=jax.ShapeDtypeStruct((OWN, D), BF16),
-        in_specs=[anywhere, vmem, vmem, anywhere, anywhere, anywhere, anywhere, vmem]
-        + [anywhere] * 4 + [vmem],
-        out_specs=vmem,
+        in_specs=[anywhere] * 13,
+        out_specs=anywhere,
         scratch_shapes=[
+            pltpu.VMEM((D,), F32),
+            pltpu.VMEM((1, HD), F32),
+            pltpu.VMEM((D,), F32),
+            pltpu.VMEM((1, ROWS), jnp.int32),
+            pltpu.VMEM((OWN, D), BF16),
             pltpu.VMEM((HEADS, OWN, D), BF16),
             pltpu.VMEM((ROWS, D), F32),
             pltpu.VMEM((FEATS, D), BF16),
@@ -297,7 +336,7 @@
             pltpu.VMEM((PEERS * OWN, D), F32),
             pltpu.VMEM((PEERS, OWN, D), BF16),
             pltpu.VMEM((PEERS, OWN, D), BF16),
-            dma((7,)), dma((4,)), dma((4,)),
+            dma((8,)), dma((4,)), dma((4,)), dma((4,)), pltpu.SemaphoreType.REGULAR((2,)),
             dma((HEADS,)), dma((HEADS,)), dma((HEADS,)), dma((HEADS,)),
             dma((PEERS,)), dma((PEERS,)), dma((PEERS,)), dma((PEERS,)),
             dma((4,)), dma((4,)),
@@ -307,8 +346,8 @@
         ),
         name="decode_layer",
     )(
-        tokens, norm_attn.reshape(1, D), query_scale.reshape(1, HD), w_query, w_key, w_value, w_out,
-        norm_mlp.reshape(1, D), w_up, w_down, cache_k.reshape(ROWS * FEATS, CACHE),
+        tokens, norm_attn, query_scale.reshape(1, HD), w_query, w_key, w_value, w_out,
+        norm_mlp, w_up, w_down, cache_k.reshape(ROWS * FEATS, CACHE),
         cache_v.reshape(ROWS * FEATS, CACHE), lengths.reshape(1, ROWS),
     )
 

time: 37.9 us -> 36.7 us (0.968)
  local copies, waits for them, and re-layouts: 3.89 us -> 1.31 us
  Pallas kernels: 33.8 us -> 35.2 us
    reshape x2 -> x0, local copies, waits for them, and re-layouts: 2.58 us -> none  [the longest x1 1.29 us: shards(): norm_attn.reshape(1, D)]
    pallas_call x1, Pallas kernels: 33.8 us -> 35.2 us  [shards(): pl.pallas_call(layer, out_shape=jax.ShapeDtypeStruct((OWN, D), BF16), in_...]
where the time goes in v2:
time: 36.7 us; the launch traced here: 36.5 us
  Pallas kernels  35.2 us (96%)
  local copies, waits for them, and re-layouts  1.31 us (4%)
    pallas_call x1, Pallas kernels, shards(): pl.pallas_call(layer, out_shape=jax.ShapeDtypeStruct((OWN, D), BF16), in_...  35.2 us
    unnamed x1, local copies, waits for them, and re-layouts  1.31 us

profile of v2, /device:TPU:1, one launch (start us, length us, event | category | flops | bytes accessed | tf_op | source)
XLA Modules:
  0.0 36.5 jit_solution(2439376847714994955)
XLA Ops:
  0.0 35.2 %decode_layer.1 = bf16[4,1280]{1,0:T(4,128)(2,1)} custom-call(bf16[4,1280]{1,0:T(4,128)(2,1)} %tok_hbm.1, f32[1280]{0:T(1024)} %gain_attn_hbm.1, f32[1,80]{1,0:T(1,128)} %bitcast.6, bf16[160,1280]{1,0:T(8,128)(2,1)} %wq_hbm.1, bf16[160,1280]{1,0:T(8,128)(2,1)} %wk_hbm.1, bf16[160,1280]{1,0:T(8,128)(2,1)} %wv_hbm.1, bf16[160,1280]{1,0:T(8,128)(2,1)} %wo_hbm.1, ...), custom_call_target="tpu_custom_call" | custom-call | tf_op jit(solution)/shard_map/decode_layer/pallas_call | solution.py:310
  35.2 1.3 %copy.15 = bf16[4,1280]{1,0:T(4,128)(2,1)} copy(bf16[4,1280]{1,0:T(4,128)(2,1)} %decode_layer.1) | data formatting | bytes 20480

commit v3 on v2

--- a/solution.py
+++ b/solution.py
@@ -13,8 +13,9 @@
 CACHE = 512
 OWN = 4
 HEADS = 8
-PEERS = 16
+PEERS = 8
 UNITS = 40
+SHARDS = 4
 F32 = jnp.float32
 BF16 = jnp.bfloat16
 
@@ -34,12 +35,12 @@
 
 def layer(
     tok_hbm, gain_attn_hbm, scale_hbm, wq_hbm, wk_hbm, wv_hbm, wo_hbm, gain_mlp_hbm, wu_hbm, wd_hbm,
-    ck_hbm, cv_hbm, lens_hbm, out_hbm,
-    gain_attn_ref, scale_ref, gain_mlp_ref, lens_ref, out_ref,
+    ck_hbm, cv_hbm, lens_hbm, out_ref,
+    gain_attn_ref, scale_ref, gain_mlp_ref, lens_ref,
     tok_buf, rows_buf, wq_buf, wk_buf, wv_buf, wo_buf, k_buf, v_buf, wu_buf, wd_buf, spread_buf, att_buf,
     part_send, part_recv, nm_buf, nm_rows, ff_send, ff_recv,
     load_sem, small_sem, k_sem, v_sem, ready_sem,
-    tok_ssem, tok_rsem, part_ssem, part_rsem, nm_ssem, nm_rsem, ff_ssem, ff_rsem, w_ssem, w_rsem,
+    tok_ssem, tok_rsem, part_ssem, part_rsem, nm_ssem, nm_rsem, ff_ssem, ff_rsem, wu_ssem, wu_rsem, wd_ssem, wd_rsem,
 ):
     me_req = lax.axis_index("req")
     me_head = lax.axis_index("head")
@@ -47,28 +48,39 @@
     z = me_req % 8
     y = me_head // 2
     core = me_head % 2
-    place = x * 4 + (z % 2) * 2 + core
+    place = x * 2 + core
 
     def head_peer(k):
         return (me_req, (me_head + k) % HEADS)
 
     def near_peer(k):
         at = (place + k) % PEERS
-        return ((at // 4) * 8 + (z // 2) * 2 + (at // 2) % 2, y * 2 + at % 2)
-
-    def z_peer(k, at_core):
-        return (x * 8 + (z + k) % 8, y * 2 + at_core)
-
-    later = (z < 6, z < 2)
+        return ((at // 2) * 8 + z, y * 2 + at % 2)
+
+    away = 2 - core
+
+    def z_peer(n):
+        at_z = (z + (away, 8 - away, 1, 7)[n]) % 8
+        at_core = core if n < 2 else 1 - core
+        return (x * 8 + at_z, y * 2 + at_core), at_z
+
+    def start(at_z):
+        return jnp.minimum(at_z, 4)
+
+    later = [start(z_peer(n)[1]) > start(z) for n in range(4)]
+    earlier = [start(z_peer(n)[1]) < start(z) for n in range(4)]
+    expected = HEADS - 1 + PEERS - 1
+    for n in range(4):
+        expected = expected + 1 - later[n].astype(jnp.int32)
     barrier = pltpu.get_barrier_semaphore()
     for k in range(1, HEADS):
         pl.semaphore_signal(barrier, inc=1, device_id=head_peer(k), device_id_type=MESH)
     for k in range(1, PEERS):
         pl.semaphore_signal(barrier, inc=1, device_id=near_peer(k), device_id_type=MESH)
-    for n, k in enumerate((2, 6)):
-        @pl.when(later[n])
-        def _():
-            pl.semaphore_signal(barrier, inc=1, device_id=z_peer(k, 1 - core), device_id_type=MESH)
+    for n in range(4):
+        @pl.when(jnp.logical_not(earlier[n]))
+        def _():
+            pl.semaphore_signal(barrier, inc=1, device_id=z_peer(n)[0], device_id_type=MESH)
 
     load_tok = pltpu.make_async_copy(tok_hbm, tok_buf.at[me_head], load_sem.at[0])
     load_tok.start()
@@ -110,7 +122,7 @@
     )
 
     load_tok.wait()
-    pl.semaphore_wait(barrier, HEADS - 1 + PEERS - 1 + (z >= 2).astype(jnp.int32) + (z >= 6).astype(jnp.int32))
+    pl.semaphore_wait(barrier, expected)
 
     def remote(src, dst, ssem, rsem, device):
         return pltpu.make_async_remote_copy(
@@ -125,37 +137,34 @@
         copy.start()
         tok_out.append(copy)
 
-    def shard_copies(n, k):
+    def own_shard(n):
+        slot = 2 - n - core
+        device = z_peer(n)[0]
         return (
-            remote(wu_hbm, wu_buf.at[n], w_ssem.at[2 * n], w_rsem.at[2 * n], z_peer(k, 1)),
-            remote(wd_hbm, wd_buf.at[n], w_ssem.at[2 * n + 1], w_rsem.at[2 * n + 1], z_peer(k, 1)),
+            remote(wu_hbm, wu_buf.at[slot], wu_ssem.at[n], wu_rsem.at[1 - n], device),
+            remote(wd_hbm, wd_buf.at[slot], wd_ssem.at[n], wd_rsem.at[1 - n], device),
         )
 
-    def passed_on():
-        return (
-            remote(wu_buf.at[0], wu_buf.at[1], w_ssem.at[0], w_rsem.at[2], z_peer(6, 0)),
-            remote(wd_buf.at[1], wd_buf.at[1], w_ssem.at[1], w_rsem.at[3], z_peer(2, 0)),
-        )
-
-    for n, k in enumerate((2, 6)):
+    def passed_on(n):
+        four, three = z_peer(1 - n)[0], z_peer(3 - n)[0]
+        up = remote(wu_buf.at[1 + n], wu_buf.at[2 + n], wu_ssem.at[2 + n], wu_rsem.at[2 + n], three)
+        down = remote(wd_buf.at[1 + n], wd_buf.at[2 + n], wd_ssem.at[2 + n], wd_rsem.at[2 + n], three)
+        if n == 0:
+            far = remote(wu_buf.at[1], wu_buf.at[3], wu_ssem.at[4], wu_rsem.at[2], four)
+        else:
+            far = remote(wd_buf.at[2], wd_buf.at[3], wd_ssem.at[4], wd_rsem.at[2], four)
+        return far, up, down
+
+    for n in range(4):
+        @pl.when(earlier[n])
+        def _():
+            pl.semaphore_signal(ready_sem.at[n + 1 - 2 * (n % 2)], inc=1, device_id=z_peer(n)[0], device_id_type=MESH)
+
+    for n in range(2):
         @pl.when(jnp.logical_not(later[n]))
         def _():
-            pl.semaphore_signal(ready_sem.at[1 - n], inc=1, device_id=z_peer(k, 1 - core), device_id_type=MESH)
-
-            @pl.when(core == 0)
-            def _():
-                for copy in shard_copies(1 - n, k):
-                    copy.start()
-
-    def send_later(n, k):
-        @pl.when(later[n])
-        def _():
-            pl.semaphore_wait(ready_sem.at[n], 1)
-
-            @pl.when(core == 0)
-            def _():
-                for copy in shard_copies(1 - n, k):
-                    copy.start()
+            for copy in own_shard(n):
+                copy.start()
 
     @pl.when(core == 0)
     def _():
@@ -164,6 +173,13 @@
 
     for copy in tok_out:
         copy.wait_recv()
+    for n in range(2):
+        @pl.when(later[n])
+        def _():
+            pl.semaphore_wait(ready_sem.at[n], 1)
+            for copy in own_shard(n):
+                copy.start()
+
     for n in range(HEADS):
         rows_buf[pl.ds(OWN * n, OWN), :] = tok_buf[n].astype(F32)
     for copy in smalls:
@@ -188,7 +204,6 @@
     eye = lax.broadcasted_iota(jnp.int32, (ROWS, ROWS), 0) == lax.broadcasted_iota(jnp.int32, (ROWS, ROWS), 1)
     lens = jnp.sum(jnp.where(eye, jnp.broadcast_to(lens_ref[...], (ROWS, ROWS)), 0), axis=-1, keepdims=True)
 
-    send_later(0, 2)
     slot = lax.broadcasted_iota(jnp.int32, (16, CACHE), 1)
     scores = []
     for g in range(4):
@@ -231,15 +246,18 @@
         copy.start()
         part_out.append(copy)
 
-    send_later(1, 6)
-
-    @pl.when(core == 1)
-    def _():
-        for n, k in ((0, 6), (1, 2)):
-            for copy in shard_copies(n, k):
+    for n in range(2, 4):
+        @pl.when(later[n])
+        def _():
+            pl.semaphore_wait(ready_sem.at[n], 1)
+
+    @pl.when(core == 0)
+    def _():
+        for n in range(2):
+            for copy in own_shard(1 - n):
                 copy.wait_recv()
-        for copy in passed_on():
-            copy.start()
+            for copy in passed_on(n):
+                copy.start()
 
     mid = tok_buf[me_head].astype(F32)
     mid = mid + part_send[me_head].astype(F32)
@@ -257,19 +275,23 @@
     def _():
         load_wu.wait()
         load_wd.wait()
-        for copy in passed_on():
-            copy.wait_recv()
+        for n in range(2):
+            passed_on(n)[0].wait_recv()
+
+    @pl.when(core == 1)
+    def _():
+        for n in range(2):
+            for copy in own_shard(n) + passed_on(n)[1:]:
+                copy.wait_recv()
 
     for copy in nm_out:
         copy.wait_recv()
     for n in range(PEERS):
         nm_rows[pl.ds(OWN * n, OWN), :] = nm_buf[n].astype(F32)
     normed_mid = nm_rows[...].astype(BF16)
-    mixed = jnp.zeros((PEERS * OWN, D), F32)
-    for n in range(2):
-        hidden = times_rows(normed_mid, wu_buf[n])
-        hidden = (hidden / (1.0 + jnp.exp(-hidden))).astype(BF16)
-        mixed = mixed + times(hidden, wd_buf[n])
+    hidden = times_rows(normed_mid, wu_buf[...].reshape(SHARDS * UNITS, D))
+    hidden = (hidden / (1.0 + jnp.exp(-hidden))).astype(BF16)
+    mixed = times(hidden, wd_buf[...].reshape(SHARDS * UNITS, D))
     for n in range(PEERS):
         ff_send[n] = mixed[OWN * n : OWN * n + OWN].astype(BF16)
     ff_out = []
@@ -282,24 +304,19 @@
         copy.wait_recv()
         result = result + ff_recv[k].astype(F32)
     out_ref[...] = result.astype(BF16)
-    store_out = pltpu.make_async_copy(out_ref, out_hbm, load_sem.at[7])
-    store_out.start()
 
     for copy in tok_out + part_out + nm_out + ff_out:
         copy.wait_send()
 
+    for n in range(2):
+        for copy in own_shard(n):
+            copy.wait_send()
+
     @pl.when(core == 0)
     def _():
-        for n, k in ((0, 6), (1, 2)):
-            for copy in shard_copies(n, k):
+        for n in range(2):
+            for copy in passed_on(n):
                 copy.wait_send()
-
-    @pl.when(core == 1)
-    def _():
-        for copy in passed_on():
-            copy.wait_send()
-
-    store_out.wait()
 
 
 def shards(
@@ -309,15 +326,14 @@
     dma = pltpu.SemaphoreType.DMA
     return pl.pallas_call(
         layer,
-        out_shape=jax.ShapeDtypeStruct((OWN, D), BF16),
+        out_shape=pltpu.VMEM((OWN, D), BF16),
         in_specs=[anywhere] * 13,
-        out_specs=anywhere,
+        out_specs=pl.BlockSpec(memory_space=pltpu.VMEM),
         scratch_shapes=[
             pltpu.VMEM((D,), F32),
             pltpu.VMEM((1, HD), F32),
             pltpu.VMEM((D,), F32),
             pltpu.VMEM((1, ROWS), jnp.int32),
-            pltpu.VMEM((OWN, D), BF16),
             pltpu.VMEM((HEADS, OWN, D), BF16),
             pltpu.VMEM((ROWS, D), F32),
             pltpu.VMEM((FEATS, D), BF16),
@@ -326,8 +342,8 @@
             pltpu.VMEM((FEATS, D), BF16),
             pltpu.VMEM((ROWS * FEATS, CACHE), BF16),
             pltpu.VMEM((ROWS * FEATS, CACHE), BF16),
-            pltpu.VMEM((2, UNITS, D), BF16),
-            pltpu.VMEM((2, UNITS, D), BF16),
+            pltpu.VMEM((SHARDS, UNITS, D), BF16),
+            pltpu.VMEM((SHARDS, UNITS, D), BF16),
             pltpu.VMEM((FEATS, D), BF16),
             pltpu.VMEM((ROWS, D), F32),
             pltpu.VMEM((HEADS, OWN, D), BF16),
@@ -336,10 +352,10 @@
             pltpu.VMEM((PEERS * OWN, D), F32),
             pltpu.VMEM((PEERS, OWN, D), BF16),
             pltpu.VMEM((PEERS, OWN, D), BF16),
-            dma((8,)), dma((4,)), dma((4,)), dma((4,)), pltpu.SemaphoreType.REGULAR((2,)),
+            dma((7,)), dma((4,)), dma((4,)), dma((4,)), pltpu.SemaphoreType.REGULAR((4,)),
             dma((HEADS,)), dma((HEADS,)), dma((HEADS,)), dma((HEADS,)),
             dma((PEERS,)), dma((PEERS,)), dma((PEERS,)), dma((PEERS,)),
-            dma((4,)), dma((4,)),
+            dma((5,)), dma((4,)), dma((5,)), dma((4,)),
         ],
         compiler_params=pltpu.CompilerParams(
             collective_id=0, has_side_effects=True, vmem_limit_bytes=60 * 1024 * 1024

time: 36.7 us -> 32.8 us (0.89)
  Pallas kernels: 35.2 us -> 32.1 us
  local copies, waits for them, and re-layouts: 1.31 us -> 0.6 us
    pallas_call x1, Pallas kernels: 35.2 us -> 32.1 us  [shards(): pl.pallas_call(layer, out_shape=pltpu.VMEM((OWN, D), BF16), in_specs=[any...]
    unnamed x1, local copies, waits for them, and re-layouts: 1.31 us -> 0.6 us
where the time goes in v3:
time: 32.8 us; the launch traced here: 32.7 us
  Pallas kernels  32.1 us (98%)
  local copies, waits for them, and re-layouts  0.6 us (2%)
    pallas_call x1, Pallas kernels, shards(): pl.pallas_call(layer, out_shape=pltpu.VMEM((OWN, D), BF16), in_specs=[any...  32.1 us

profile of v3, /device:TPU:1, one launch (start us, length us, event | category | flops | bytes accessed | tf_op | source)
XLA Modules:
  0.0 32.7 jit_solution(10604518423893031667)
XLA Ops:
  0.0 32.1 %decode_layer.1 = bf16[4,1280]{1,0:T(4,128)(2,1)S(1)} custom-call(bf16[4,1280]{1,0:T(4,128)(2,1)} %tok_hbm.1, f32[1280]{0:T(1024)} %gain_attn_hbm.1, f32[1,80]{1,0:T(1,128)} %bitcast.6, bf16[160,1280]{1,0:T(8,128)(2,1)} %wq_hbm.1, bf16[160,1280]{1,0:T(8,128)(2,1)} %wk_hbm.1, bf16[160,1280]{1,0:T(8,128)(2,1)} %wv_hbm.1, bf16[160,1280]{1,0:T(8,128)(2,1)} %wo_hbm.1, ...), custom_call_target="tpu_custom_call" | custom-call | tf_op jit(solution)/shard_map/decode_layer/pallas_call | solution.py:327
  32.1 0.6 %copy.15 = bf16[4,1280]{1,0:T(4,128)(2,1)} copy(bf16[4,1280]{1,0:T(4,128)(2,1)S(1)} %decode_layer.1) | data formatting | bytes 20480

commit v4 on v3

--- a/solution.py
+++ b/solution.py
@@ -37,53 +37,64 @@
     tok_hbm, gain_attn_hbm, scale_hbm, wq_hbm, wk_hbm, wv_hbm, wo_hbm, gain_mlp_hbm, wu_hbm, wd_hbm,
     ck_hbm, cv_hbm, lens_hbm, out_ref,
     gain_attn_ref, scale_ref, gain_mlp_ref, lens_ref,
-    tok_buf, rows_buf, wq_buf, wk_buf, wv_buf, wo_buf, k_buf, v_buf, wu_buf, wd_buf, spread_buf, att_buf,
+    tok_buf, rows_buf, wq_buf, wk_buf, wv_buf, wo_buf, k_buf, v_buf, w_buf, spread_buf, att_buf,
     part_send, part_recv, nm_buf, nm_rows, ff_send, ff_recv,
     load_sem, small_sem, k_sem, v_sem, ready_sem,
-    tok_ssem, tok_rsem, part_ssem, part_rsem, nm_ssem, nm_rsem, ff_ssem, ff_rsem, wu_ssem, wu_rsem, wd_ssem, wd_rsem,
+    tok_ssem, tok_rsem, part_ssem, part_rsem, nm_ssem, nm_rsem, ff_ssem, ff_rsem, w_ssem, w_rsem, pair_ssem, pair_rsem,
 ):
     me_req = lax.axis_index("req")
     me_head = lax.axis_index("head")
-    x = me_req // 8
-    z = me_req % 8
-    y = me_head // 2
-    core = me_head % 2
-    place = x * 2 + core
+    x = lax.div(me_req, 8)
+    z = lax.rem(me_req, 8)
+    core = lax.rem(me_head, 2)
+    z_odd = lax.rem(z, 2)
+    z_twin = z + 1 - 2 * z_odd
 
     def head_peer(k):
-        return (me_req, (me_head + k) % HEADS)
+        return (me_req, lax.rem(me_head + k, HEADS))
 
     def near_peer(k):
-        at = (place + k) % PEERS
-        return ((at // 2) * 8 + z, y * 2 + at % 2)
-
-    away = 2 - core
+        return (lax.rem(x + k % 4, 4) * 8 + (z if k < 4 else z_twin), me_head)
+
+    def near_back(k):
+        return (4 - k) % 4 + 4 * (k // 4)
+
+    away = (2 + 4 * core, 6 - 4 * core)
 
     def z_peer(n):
-        at_z = (z + (away, 8 - away, 1, 7)[n]) % 8
-        at_core = core if n < 2 else 1 - core
-        return (x * 8 + at_z, y * 2 + at_core), at_z
+        return (x * 8 + lax.rem(z + away[n], 8), me_head)
+
+    other_core = (me_req, me_head + 1 - 2 * core)
 
     def start(at_z):
         return jnp.minimum(at_z, 4)
 
-    later = [start(z_peer(n)[1]) > start(z) for n in range(4)]
-    earlier = [start(z_peer(n)[1]) < start(z) for n in range(4)]
-    expected = HEADS - 1 + PEERS - 1
-    for n in range(4):
-        expected = expected + 1 - later[n].astype(jnp.int32)
+    later = [start(lax.rem(z + away[n], 8)) > start(z) for n in range(2)]
+    earlier = [start(lax.rem(z + away[n], 8)) < start(z) for n in range(2)]
+    twin_later = start(z_twin) > start(z)
+    twin_earlier = start(z_twin) < start(z)
+    load_tok = pltpu.make_async_copy(tok_hbm, tok_buf.at[me_head], load_sem.at[0])
+    load_tok.start()
     barrier = pltpu.get_barrier_semaphore()
     for k in range(1, HEADS):
         pl.semaphore_signal(barrier, inc=1, device_id=head_peer(k), device_id_type=MESH)
-    for k in range(1, PEERS):
+    for k in range(1, 4):
         pl.semaphore_signal(barrier, inc=1, device_id=near_peer(k), device_id_type=MESH)
-    for n in range(4):
+    expected = HEADS - 1 + 3
+    for n in range(2):
+        expected = expected + 1 - later[n].astype(jnp.int32)
+
         @pl.when(jnp.logical_not(earlier[n]))
         def _():
-            pl.semaphore_signal(barrier, inc=1, device_id=z_peer(n)[0], device_id_type=MESH)
-
-    load_tok = pltpu.make_async_copy(tok_hbm, tok_buf.at[me_head], load_sem.at[0])
-    load_tok.start()
+            pl.semaphore_signal(barrier, inc=1, device_id=z_peer(n), device_id_type=MESH)
+
+    expected = expected + 4 - 4 * twin_later.astype(jnp.int32)
+
+    @pl.when(jnp.logical_not(twin_earlier))
+    def _():
+        for k in range(4, PEERS):
+            pl.semaphore_signal(barrier, inc=1, device_id=near_peer(k), device_id_type=MESH)
+
     smalls = []
     for n, (src, dst) in enumerate((
         (gain_attn_hbm, gain_attn_ref), (scale_hbm, scale_ref), (lens_hbm, lens_ref), (gain_mlp_hbm, gain_mlp_ref)
@@ -95,6 +106,10 @@
         loads.append(pltpu.make_async_copy(src, dst, load_sem.at[1 + n]))
         loads[-1].start()
     load_k, load_v = [], []
+    load_wu = pltpu.make_async_copy(wu_hbm, w_buf.at[0, 0], load_sem.at[5])
+    load_wu.start()
+    load_wd = pltpu.make_async_copy(wd_hbm, w_buf.at[1, 0], load_sem.at[6])
+    load_wd.start()
     for g in range(4):
         rows = pl.ds(g * D, D)
         load_k.append(pltpu.make_async_copy(ck_hbm.at[rows], k_buf.at[rows], k_sem.at[g]))
@@ -105,8 +120,6 @@
         load_v[-1].start()
     load_wo = pltpu.make_async_copy(wo_hbm, wo_buf, load_sem.at[4])
     load_wo.start()
-    load_wu = pltpu.make_async_copy(wu_hbm, wu_buf.at[0], load_sem.at[5])
-    load_wd = pltpu.make_async_copy(wd_hbm, wd_buf.at[0], load_sem.at[6])
 
     column = lax.broadcasted_iota(jnp.int32, (1, D), 1)
     block = jnp.zeros((1, D), jnp.int32)
@@ -137,39 +150,33 @@
         copy.start()
         tok_out.append(copy)
 
-    def own_shard(n):
-        slot = 2 - n - core
-        device = z_peer(n)[0]
-        return (
-            remote(wu_hbm, wu_buf.at[slot], wu_ssem.at[n], wu_rsem.at[1 - n], device),
-            remote(wd_hbm, wd_buf.at[slot], wd_ssem.at[n], wd_rsem.at[1 - n], device),
-        )
-
-    def passed_on(n):
-        four, three = z_peer(1 - n)[0], z_peer(3 - n)[0]
-        up = remote(wu_buf.at[1 + n], wu_buf.at[2 + n], wu_ssem.at[2 + n], wu_rsem.at[2 + n], three)
-        down = remote(wd_buf.at[1 + n], wd_buf.at[2 + n], wd_ssem.at[2 + n], wd_rsem.at[2 + n], three)
-        if n == 0:
-            far = remote(wu_buf.at[1], wu_buf.at[3], wu_ssem.at[4], wu_rsem.at[2], four)
-        else:
-            far = remote(wd_buf.at[2], wd_buf.at[3], wd_ssem.at[4], wd_rsem.at[2], four)
-        return far, up, down
-
-    for n in range(4):
+    slots = (1 + core, 2 - core)
+    own_shard = [
+        remote(w_buf.at[core, 0], w_buf.at[core, slots[1 - n]], w_ssem.at[n], w_rsem.at[1 - n], z_peer(n))
+        for n in range(2)
+    ]
+    passed_on = remote(w_buf.at[core, slots[0]], w_buf.at[core, 3], w_ssem.at[2], w_rsem.at[2], z_peer(1))
+
+    def to_other_core(n):
+        at = w_buf.at[core, (slots[0], slots[1], 3)[n]]
+        return remote(at, at, pair_ssem.at[n], pair_rsem.at[n], other_core)
+
+    for n in range(2):
         @pl.when(earlier[n])
         def _():
-            pl.semaphore_signal(ready_sem.at[n + 1 - 2 * (n % 2)], inc=1, device_id=z_peer(n)[0], device_id_type=MESH)
-
+            pl.semaphore_signal(ready_sem.at[1 - n], inc=1, device_id=z_peer(n), device_id_type=MESH)
+
+    @pl.when(twin_earlier)
+    def _():
+        for k in range(4, PEERS):
+            pl.semaphore_signal(ready_sem.at[2], inc=1, device_id=near_peer(k), device_id_type=MESH)
+
+    load_wu.wait()
+    load_wd.wait()
     for n in range(2):
         @pl.when(jnp.logical_not(later[n]))
         def _():
-            for copy in own_shard(n):
-                copy.start()
-
-    @pl.when(core == 0)
-    def _():
-        load_wu.start()
-        load_wd.start()
+            own_shard[n].start()
 
     for copy in tok_out:
         copy.wait_recv()
@@ -177,8 +184,7 @@
         @pl.when(later[n])
         def _():
             pl.semaphore_wait(ready_sem.at[n], 1)
-            for copy in own_shard(n):
-                copy.start()
+            own_shard[n].start()
 
     for n in range(HEADS):
         rows_buf[pl.ds(OWN * n, OWN), :] = tok_buf[n].astype(F32)
@@ -211,6 +217,11 @@
         load_k[g].wait()
         left = jnp.concatenate([jnp.where(mask, spread_query[at], 0.0) for mask in masks], axis=0)
         scores.append(times(left.astype(BF16), k_buf[pl.ds(g * D, D), :]))
+    own_shard[1].wait_recv()
+    passed_on.start()
+    to_other_core(0).start()
+    own_shard[0].wait_recv()
+    to_other_core(1).start()
     probs, prob_new, total = [], [], []
     for g in range(4):
         at = slice(8 * g, 8 * g + 8)
@@ -246,18 +257,9 @@
         copy.start()
         part_out.append(copy)
 
-    for n in range(2, 4):
-        @pl.when(later[n])
-        def _():
-            pl.semaphore_wait(ready_sem.at[n], 1)
-
-    @pl.when(core == 0)
+    @pl.when(twin_later)
     def _():
-        for n in range(2):
-            for copy in own_shard(1 - n):
-                copy.wait_recv()
-            for copy in passed_on(n):
-                copy.start()
+        pl.semaphore_wait(ready_sem.at[2], 4)
 
     mid = tok_buf[me_head].astype(F32)
     mid = mid + part_send[me_head].astype(F32)
@@ -271,32 +273,23 @@
         copy.start()
         nm_out.append(copy)
 
-    @pl.when(core == 0)
-    def _():
-        load_wu.wait()
-        load_wd.wait()
-        for n in range(2):
-            passed_on(n)[0].wait_recv()
-
-    @pl.when(core == 1)
-    def _():
-        for n in range(2):
-            for copy in own_shard(n) + passed_on(n)[1:]:
-                copy.wait_recv()
-
+    passed_on.wait_recv()
+    to_other_core(2).start()
+    for n in range(3):
+        to_other_core(n).wait_recv()
     for copy in nm_out:
         copy.wait_recv()
     for n in range(PEERS):
         nm_rows[pl.ds(OWN * n, OWN), :] = nm_buf[n].astype(F32)
     normed_mid = nm_rows[...].astype(BF16)
-    hidden = times_rows(normed_mid, wu_buf[...].reshape(SHARDS * UNITS, D))
+    hidden = times_rows(normed_mid, w_buf[0].reshape(SHARDS * UNITS, D))
     hidden = (hidden / (1.0 + jnp.exp(-hidden))).astype(BF16)
-    mixed = times(hidden, wd_buf[...].reshape(SHARDS * UNITS, D))
+    mixed = times(hidden, w_buf[1].reshape(SHARDS * UNITS, D))
     for n in range(PEERS):
         ff_send[n] = mixed[OWN * n : OWN * n + OWN].astype(BF16)
     ff_out = []
     for k in range(1, PEERS):
-        copy = remote(ff_send.at[PEERS - k], ff_recv.at[k], ff_ssem.at[k], ff_rsem.at[k], near_peer(k))
+        copy = remote(ff_send.at[near_back(k)], ff_recv.at[k], ff_ssem.at[k], ff_rsem.at[k], near_peer(k))
         copy.start()
         ff_out.append(copy)
     result = mid + ff_send[0].astype(F32)
@@ -308,15 +301,8 @@
     for copy in tok_out + part_out + nm_out + ff_out:
         copy.wait_send()
 
-    for n in range(2):
-        for copy in own_shard(n):
-            copy.wait_send()
-
-    @pl.when(core == 0)
-    def _():
-        for n in range(2):
-            for copy in passed_on(n):
-                copy.wait_send()
+    for copy in (*own_shard, passed_on, *(to_other_core(n) for n in range(3))):
+        copy.wait_send()
 
 
 def shards(
@@ -342,8 +328,7 @@
             pltpu.VMEM((FEATS, D), BF16),
             pltpu.VMEM((ROWS * FEATS, CACHE), BF16),
             pltpu.VMEM((ROWS * FEATS, CACHE), BF16),
-            pltpu.VMEM((SHARDS, UNITS, D), BF16),
-            pltpu.VMEM((SHARDS, UNITS, D), BF16),
+            pltpu.VMEM((2, SHARDS, UNITS, D), BF16),
             pltpu.VMEM((FEATS, D), BF16),
             pltpu.VMEM((ROWS, D), F32),
             pltpu.VMEM((HEADS, OWN, D), BF16),
@@ -352,10 +337,10 @@
             pltpu.VMEM((PEERS * OWN, D), F32),
             pltpu.VMEM((PEERS, OWN, D), BF16),
             pltpu.VMEM((PEERS, OWN, D), BF16),
-            dma((7,)), dma((4,)), dma((4,)), dma((4,)), pltpu.SemaphoreType.REGULAR((4,)),
+            dma((7,)), dma((4,)), dma((4,)), dma((4,)), pltpu.SemaphoreType.REGULAR((3,)),
             dma((HEADS,)), dma((HEADS,)), dma((HEADS,)), dma((HEADS,)),
             dma((PEERS,)), dma((PEERS,)), dma((PEERS,)), dma((PEERS,)),
-            dma((5,)), dma((4,)), dma((5,)), dma((4,)),
+            dma((3,)), dma((3,)), dma((3,)), dma((3,)),
         ],
         compiler_params=pltpu.CompilerParams(
             collective_id=0, has_side_effects=True, vmem_limit_bytes=60 * 1024 * 1024

time: 32.8 us -> 33 us (level)
  no operation moved by 1% of the time
where the time goes in v4:
time: 33 us; the launch traced here: 32.8 us
  Pallas kernels  32.2 us (98%)
  local copies, waits for them, and re-layouts  0.6 us (2%)
    pallas_call x1, Pallas kernels, shards(): pl.pallas_call(layer, out_shape=pltpu.VMEM((OWN, D), BF16), in_specs=[any...  32.2 us

profile of v4, /device:TPU:1, one launch (start us, length us, event | category | flops | bytes accessed | tf_op | source)
XLA Modules:
  0.0 32.8 jit_solution(17087920390222440236)
XLA Ops:
  0.0 32.2 %decode_layer.1 = bf16[4,1280]{1,0:T(4,128)(2,1)S(1)} custom-call(bf16[4,1280]{1,0:T(4,128)(2,1)} %tok_hbm.1, f32[1280]{0:T(1024)} %gain_attn_hbm.1, f32[1,80]{1,0:T(1,128)} %bitcast.6, bf16[160,1280]{1,0:T(8,128)(2,1)} %wq_hbm.1, bf16[160,1280]{1,0:T(8,128)(2,1)} %wk_hbm.1, bf16[160,1280]{1,0:T(8,128)(2,1)} %wv_hbm.1, bf16[160,1280]{1,0:T(8,128)(2,1)} %wo_hbm.1, ...), custom_call_target="tpu_custom_call" | custom-call | tf_op jit(solution)/shard_map/decode_layer/pallas_call | solution.py:313
  32.2 0.6 %copy.15 = bf16[4,1280]{1,0:T(4,128)(2,1)} copy(bf16[4,1280]{1,0:T(4,128)(2,1)S(1)} %decode_layer.1) | data formatting | bytes 20480
